TPU v7x, 128 devices: a whole 4x4x4 slice. The times are simulated.
128 devices in a mesh: group: 8 (over y_lo, x), mp: 16 (over y_hi, z, core).
Axes of the slice: x: 4, y: 4 (y_hi: 2, y_lo: 2; y = y_hi * 2 + y_lo), z: 4, core: 2. Of those that a mesh axis runs over, the one named last changes fastest.
Arguments:
- tokens: bfloat16 [640, 4096], P(None, 'group'), may hold values from -6 to 6
- trunk_gate: bfloat16 [4096, 11008], P('group', 'mp'), may hold values from -0.09375 to 0.09375
- trunk_up: bfloat16 [4096, 11008], P('group', 'mp'), may hold values from -0.09375 to 0.09375
- trunk_down: bfloat16 [11008, 4096], P('mp', 'group'), may hold values from -0.0546875 to 0.0546875
- head_gate: bfloat16 [8, 4096, 11008], P('group', None, 'mp'), may hold values from -0.09375 to 0.09375
- head_up: bfloat16 [8, 4096, 11008], P('group', None, 'mp'), may hold values from -0.09375 to 0.09375
- head_down: bfloat16 [8, 11008, 4096], P('group', 'mp'), may hold values from -0.0546875 to 0.0546875
- head_grads: bfloat16 [8, 640, 4096], P('group', None, 'mp'), may hold values from -6 to 6
Outputs:
- grad_x: bfloat16 [640, 4096], P('mp', 'group')
- grad_gate: float32 [4096, 11008], P('group', 'mp')
- grad_up: float32 [4096, 11008], P('group', 'mp')
- grad_down: float32 [11008, 4096], P('mp', 'group')
All inputs are finite; a program needn't handle non-finite values.
Results may differ from a plain program's by a relative error of at most 0.009.
Values may be sent and summed in bfloat16 or wider, within the bound.
A program may use at most 128 MiB of HBM per device.

v0:
```python
import functools

import jax
import jax.numpy as jnp
from jax import lax
from jax.experimental import pallas as pl
from jax.experimental.pallas import tpu as pltpu
from jax.sharding import PartitionSpec as P

F32 = jnp.float32
BF16 = jnp.bfloat16
MESH = pl.DeviceIdType.MESH
D = 4096
FL = 688
FP = 768
CW = 512
TILES = ((0, 256), (256, 256), (512, 176))
FINAL = (16, 16, 8)
ROWS = tuple(16 * f for f in FINAL)


def contract_first(left, right):
    return lax.dot_general(left, right, (((0,), (0,)), ((), ())), preferred_element_type=F32)


def dot(left, right):
    return jnp.dot(left, right, preferred_element_type=F32)


def dot_t(left, right):
    return lax.dot_general(left, right, (((1,), (1,)), ((), ())), preferred_element_type=F32)


def f32(x):
    return x.astype(F32)


def chunk_scratch(rows):
    r8, r4, r2, r16 = rows // 8, rows // 4, rows // 2, rows // 16
    shapes = dict(
        P=((8, 2, r8, FL), BF16),
        hid=((8, r8, FL), BF16),
        ab=((2, 8, r8, FL), BF16),
        D3=((rows, CW), BF16),
        D3r=((r2, CW), BF16),
        to=((rows, D), BF16),
        land=((rows, D), BF16),
        dk=((rows, 2 * FP), BF16),
        cr=((r2, D), BF16),
        E5=((r2, CW), BF16),
        dt=((rows, CW), BF16),
        G7=((8, r8, FL), BF16),
        gh=((8, r8, FL), BF16),
        dgu=((2, rows, FL), BF16),
        X9=((2, 2, 4, r16, CW), BF16),
        X9r=((2, 4, r16, CW), BF16),
        own=((r16, CW), BF16),
        c3=((7, r4, 128), BF16),
        e5=((7, r4, 128), BF16),
        c9=((7, r16, CW), BF16),
    )
    shapes["c7"] = ((7, r8, FL), BF16)
    for name, shape in (("c1", (2, r8, FL)), ("c5", (r2, CW))):
        shapes[name + "_rel"] = ((2, *shape), BF16)
        shapes[name + "_rl"] = ((2, *shape), BF16)
        shapes[name + "_rr"] = ((2, *shape), BF16)
        shapes[name + "_p"] = ((2, *shape), BF16)
    return shapes


SHARED = dict(
    W=((2 * FP, D), BF16),
    Wd=((FL, D), BF16),
    tg=((FL, CW), BF16),
    tu=((FL, CW), BF16),
    td=((FL, CW), BF16),
    hg=((sum(ROWS), 256), BF16),
    cot=((sum(ROWS), D), BF16),
    ghid=((sum(ROWS), FL), F32),
)
N_SEM = 420
ORDER = (
    "0c10102c10210120c1200211c2022102c10hh2021hh0hh10001001210110",
    "12010212012212012202122012120012102210210212102",
)


def layout():
    names, shapes = [], []
    for name, (shape, dtype) in SHARED.items():
        names.append(name)
        shapes.append(pltpu.VMEM(shape, dtype))
    for c, rows in enumerate(ROWS):
        names.append(f"tok{c}")
        shapes.append(pltpu.VMEM((rows, CW), BF16))
        for name, (shape, dtype) in chunk_scratch(rows).items():
            names.append(f"{name}{c}")
            shapes.append(pltpu.VMEM(shape, dtype))
    return names, shapes


class Net:
    def __init__(self, send_sem, recv_sem, copy_sem):
        self.send_sem, self.recv_sem, self.copy_sem = send_sem, recv_sem, copy_sem
        self.n = self.k = 0
        self.sent = []

    def send(self, src, dst, dev):
        copy = pltpu.make_async_remote_copy(
            src_ref=src,
            dst_ref=dst,
            send_sem=self.send_sem.at[self.n],
            recv_sem=self.recv_sem.at[self.n],
            device_id=dev,
            device_id_type=MESH,
        )
        self.n += 1
        copy.start()
        self.sent.append(copy)
        return copy

    def copy(self, src, dst):
        copy = pltpu.make_async_copy(src, dst, self.copy_sem.at[self.k])
        self.k += 1
        copy.start()
        return copy


def kernel(names, *refs):
    (tokens, tgate, tup, tdown, hgate, hup, hdown, hgrads, *rest) = refs
    outs, rest = rest[:4], rest[4:]
    S = dict(zip(names, rest[: len(names)], strict=True))
    net = Net(*rest[len(names) :])
    send = net.send

    g, m = lax.axis_index("group"), lax.axis_index("mp")
    yl, x = lax.div(g, 4), lax.rem(g, 4)
    yh, z, core = lax.div(m, 8), lax.rem(lax.div(m, 2), 4), lax.rem(m, 2)

    def ring(i, step):
        return lax.rem(i + step, 4)

    xr, xl = (yl * 4 + ring(x, 1), m), (yl * 4 + ring(x, 3), m)
    zr, zl = (g, yh * 8 + ring(z, 1) * 2 + core), (g, yh * 8 + ring(z, 3) * 2 + core)
    lp = ((1 - yl) * 4 + x, m)
    hp = (g, (1 - yh) * 8 + z * 2 + core)
    cp = (g, m + 1 - 2 * core)

    def across(dh, dx=0, dz=0):
        return (yl * 4 + ring(x, dx), lax.rem(yh + dh, 2) * 8 + ring(z, dz) * 2 + core)

    far_z = [(dh, dz, across(dh, dz=dz)) for dh in (0, 1) for dz in range(4) if dh or dz]
    far_x = [(dh, dx, across(dh, dx=dx)) for dh in (0, 1) for dx in range(4) if dh or dx]
    far_g = [
        (dh, dx, (lax.rem(yl + dh, 2) * 4 + ring(x, dx), m)) for dx in (1, 3, 2, 0) for dh in (0, 1) if dh or dx
    ]
    near = [dev for _, _, dev in far_g] + [zr, zl, hp, cp, across(0, dz=2)]
    near += [across(1, dx=i) for i in (1, 2, 3)] + [across(1, dz=i) for i in (1, 2, 3)]

    w_tok = [
        [
            net.copy(tokens.at[pl.ds(i * sum(FINAL) + sum(FINAL[:c]), f)], S[f"tok{c}"].at[pl.ds(i * f, f)])
            for i in range(16)
        ]
        for c, f in enumerate(FINAL)
    ]
    w_tg, w_tu = net.copy(tgate, S["tg"]), net.copy(tup, S["tu"])
    w_hg = [
        net.copy(
            hgrads.at[pl.ds(i * sum(FINAL) + sum(FINAL[:c]), f)], S["hg"].at[pl.ds(sum(ROWS[:c]) + i * f, f)]
        )
        for c, f in enumerate(FINAL)
        for i in range(16)
    ]
    w_td = net.copy(tdown, S["td"])
    w_hd = net.copy(hdown, S["Wd"])
    w_h = [
        net.copy(
            src.at[:, pl.ds((j * 4 + i) * 128, 128)],
            S["W"].at[pl.ds(top, FL), pl.ds((i * 8 + j % 4 * 2 + j // 4) * 128, 128)],
        )
        for src, top in ((hgate, 0), (hup, FP))
        for i in range(4)
        for j in range(8)
    ]
    for top in (FL, FP + FL):
        S["W"][top : top + FP - FL, :] = jnp.zeros((FP - FL, D), BF16)
    for c, rows in enumerate(ROWS):
        for last in (FP, 2 * FP):
            S[f"dk{c}"][:, last - 128 : last] = jnp.zeros((rows, 128), BF16)

    barrier = pltpu.get_barrier_semaphore()
    for dev in near:
        pl.semaphore_signal(barrier, inc=1, device_id=dev, device_id_type=MESH)

    def acc(dst, src):
        dst[...] = (f32(dst[...]) + f32(src[...])).astype(BF16)

    def rs_tail(win, bufs, r, devs, h, pdev, a, b, c1=None, d0=None, before_sum=None):
        rel, rl, rr, p = bufs
        rdev, ldev = devs
        yield
        a.wait_recv()
        acc(win(0, ring(r, 1)), rel.at[0])
        c0 = send(win(0, ring(r, 1)), rl.at[0], rdev)
        b.wait_recv()
        acc(win(1, ring(r, 3)), rel.at[1])
        d1 = send(win(1, ring(r, 3)), rr.at[1], ldev)
        if c1 is None:
            c1 = send(win(1, ring(r, 1)), rl.at[1], rdev)
            d0 = send(win(0, ring(r, 3)), rr.at[0], ldev)
        if before_sum is not None:
            before_sum()
        yield
        for copy in (c1, d0, c0, d1):
            copy.wait_recv()
        oh = 1 - h
        p[0] = (f32(win(oh, r)[...]) + f32(rl[oh]) + f32(rr[oh])).astype(BF16)
        q = send(p.at[0], p.at[1], pdev)
        yield
        q.wait_recv()
        return f32(win(h, r)[...]) + f32(rl[h]) + f32(rr[h]) + f32(p[1])

    def rs(win, bufs, r, devs, h, pdev):
        rel, rl, rr, _ = bufs
        rdev, ldev = devs
        a = send(win(0, ring(r, 2)), rel.at[0], rdev)
        b = send(win(1, ring(r, 2)), rel.at[1], ldev)
        return (yield from rs_tail(win, bufs, r, devs, h, pdev, a, b))

    def ag(win, r, devs, h, pdev, have=lambda h, r: None):
        rdev, ldev = devs
        R, L, O = ring(r, 1), ring(r, 3), ring(r, 2)

        def go(h, r, dev):
            return send(win(h, r), win(h, r), dev)

        p, a1, b1 = go(h, r, pdev), go(h, r, rdev), go(h, r, ldev)
        have(h, r)
        yield
        p.wait_recv()
        a2, b2 = go(1 - h, r, rdev), go(1 - h, r, ldev)
        have(1 - h, r)
        yield
        a1.wait_recv()
        b1.wait_recv()
        have(h, L)
        have(h, R)
        a2.wait_recv()
        fr = go(0, L, rdev)
        b2.wait_recv()
        fl = go(1, R, ldev)
        have(1 - h, L)
        have(1 - h, R)
        yield
        fr.wait_recv()
        fl.wait_recv()
        have(0, O)
        have(1, O)

    cot_sent = []

    def rs_far(win, buf, h, r, far):
        copies = [send(win(lax.rem(h + dh, 2), ring(r, dr)), buf.at[i], dev) for i, (dh, dr, dev) in enumerate(far)]
        yield
        total = f32(win(h, r)[...])
        for i, copy in enumerate(copies):
            copy.wait_recv()
            total += f32(buf[i])
        return total

    def ag_far(win, h, r, far):
        copies = [send(win(h, r), win(h, r), dev) for _, _, dev in far]
        yield
        for copy in copies:
            copy.wait_recv()

    def gather_cot():
        cot, half = S["cot"], sum(ROWS) // 2

        def win(h, zz, cc=core, rows=None):
            cols = pl.ds(pl.multiple_of((h * 8 + zz * 2 + cc) * 256, 256), 256)
            return cot.at[:, cols] if rows is None else cot.at[pl.ds(rows, half), cols]

        to_core = []

        def go(src, dst, dev):
            copy = send(src, dst, dev)
            cot_sent.append(net.sent.pop())
            return copy

        def have(h, zz):
            to_core.append(go(win(h, zz), win(h, zz), cp))

        def both(h, zz, dev):
            return go(win(h, zz), win(h, zz), dev)

        mine = win(yh, z)
        for copy in w_hg:
            copy.wait()
        keep = net.copy(S["hg"], mine)
        p, a1, b1, k = (go(S["hg"], mine, dev) for dev in (hp, zr, zl, cp))
        to_core.append(k)
        yield
        p.wait_recv()
        a2, b2 = both(1 - yh, z, zr), both(1 - yh, z, zl)
        have(1 - yh, z)
        keep.wait()
        yield
        a1.wait_recv()
        b1.wait_recv()
        L, R, O = ring(z, 3), ring(z, 1), ring(z, 2)
        f1 = go(win(yh, L, rows=0), win(yh, L, rows=0), zr)
        e1 = go(win(yh, R, rows=half), win(yh, R, rows=half), zl)
        have(yh, L)
        have(yh, R)
        yield
        a2.wait_recv()
        b2.wait_recv()
        f2 = go(win(1 - yh, L, rows=0), win(1 - yh, L, rows=0), zr)
        e2 = go(win(1 - yh, R, rows=half), win(1 - yh, R, rows=half), zl)
        have(1 - yh, L)
        have(1 - yh, R)
        yield
        f1.wait_recv()
        e1.wait_recv()
        have(yh, O)
        f2.wait_recv()
        e2.wait_recv()
        have(1 - yh, O)
        for copy in to_core:
            copy.wait_recv()

    def head_hidden():
        w_hd.wait()
        row = 0
        for rows in ROWS:
            for n, w in ((0, 512), (512, 176)):
                S["ghid"][row : row + rows, n : n + w] = dot_t(S["cot"][row : row + rows, :], S["Wd"][n : n + w, :])
                yield
            row += rows

    reached = set()

    def once(key, copies=()):
        if key in reached:
            return False
        reached.add(key)
        for copy in copies:
            copy.wait()
        return True

    def chunk(c):
        rows = ROWS[c]
        row0 = sum(ROWS[:c])
        r8, r4, r2, r16 = rows // 8, rows // 4, rows // 2, rows // 16
        B = {n[:-1]: r for n, r in S.items() if n.endswith(str(c))}
        bufs = {n: tuple(B[n + e] for e in ("_rel", "_rl", "_rr", "_p")) for n in ("c1", "c5")}
        xdev, zdev = (xr, xl), (zr, zl)
        on_z = c != 1
        if on_z:
            small, far_small, big, big_dev = x, far_x, z, zdev
        else:
            small, far_small, big, big_dev = z, far_z, x, xdev

        def half(cc):
            return pl.ds(pl.multiple_of(cc * r2, r2), r2)

        def quarter(cc, h):
            return pl.ds(pl.multiple_of(cc * r2 + h * r4, r4), r4)

        def cols(i, w):
            return pl.ds(pl.multiple_of(i * w, w), w)

        for copy in w_tok[c]:
            copy.wait()
        once("gate", [w_tg, w_tu])
        for i, w_ref in enumerate((S["tg"], S["tu"])):
            for n, w in TILES:
                part = dot_t(B["tok"][...], w_ref[n : n + w, :])
                for j in range(8):
                    B["P"][j, i, :, n : n + w] = part[j * r8 : (j + 1) * r8].astype(BF16)
        yield
        total = yield from rs(lambda h, r: B["P"].at[h * 4 + r], bufs["c1"], x, xdev, yl, lp)
        hid, ab = B["hid"], B["ab"]
        gate, up = total[0], total[1]
        sig = jax.nn.sigmoid(gate)
        hid[g] = (gate * sig * up).astype(BF16)
        factors = ag(lambda h, r: ab.at[:, h * 4 + r], x, xdev, yl, lp)
        ab[0, g] = (up * (sig * (1.0 + gate * (1.0 - sig)))).astype(BF16)
        ab[1, g] = (gate * sig).astype(BF16)
        yield from ag(lambda h, r: hid.at[h * 4 + r], x, xdev, yl, lp)
        once("down", [w_td])
        B["D3"][...] = dot(hid[...].reshape(rows, FL), S["td"][...]).astype(BF16)
        k = send(B["D3"].at[half(1 - core)], B["D3r"], cp)
        next(factors)
        yield
        k.wait_recv()
        acc(B["D3"].at[half(core)], B["D3r"])
        total = yield from rs_far(lambda h, r: B["D3"].at[quarter(core, h), cols(r, 128)], B["c3"], yh, z, far_z)
        to = B["to"]
        land = B["land"]
        own = f32(B["tok"][quarter(core, yh), cols(z, 128)])

        def small_win(h, r):
            block = z * 8 + yl * 4 + r if on_z else (yl * 4 + x) * 4 + r
            return land.at[quarter(core, h), cols(block, 128)]

        def big_win(h, r):
            return land.at[half(core), cols(r * 2 + h if on_z else h * 4 + r, 512)]

        small_win(yh, small)[...] = (own + total).astype(BF16)
        yield from ag_far(small_win, yh, small, far_small)
        to_core = []

        def have(h, r):
            to_core.append(send(big_win(h, r), big_win(h, r), cp))

        yield from ag(big_win, big, big_dev, yl, lp, have)
        next(factors)
        yield
        for copy in to_core:
            copy.wait_recv()
        for zz in range(4):
            for g_x in range(4):
                for g_y in range(2):
                    i = zz * 8 + g_x * 2 + g_y
                    j = zz * 8 + g_y * 4 + g_x if on_z else (g_y * 4 + g_x) * 4 + zz
                    to[:, i * 128 : i * 128 + 128] = land[:, j * 128 : j * 128 + 128]
        next(factors)
        yield "in"
        once("head", w_h)
        for n, w in TILES:
            pair = dot_t(to[...], jnp.concatenate([S["W"][n : n + 256, :], S["W"][FP + n : FP + n + 256, :]]))
            pre, lin = pair[:, :w], pair[:, 256 : 256 + w]
            grad = S["ghid"][row0 : row0 + rows, n : n + w]
            sig = jax.nn.sigmoid(pre)
            B["dk"][:, n : n + w] = (grad * lin * (sig * (1.0 + pre * (1.0 - sig)))).astype(BF16)
            B["dk"][:, FP + n : FP + n + w] = (grad * (pre * sig)).astype(BF16)
            yield "tile"
        for _ in factors:
            pass
        dp = S["cot"]
        while cot_sent:
            cot_sent.pop().wait_send()

        def dhalf(cc):
            return pl.ds(pl.multiple_of(row0 + cc * r2, 64), r2)

        order = (ring(big, 2), ring(big, 1), ring(big, 3), big)
        ks = []

        def dcols(r, h):
            return cols(r * 2 + h if on_z else h * 4 + r, 512)

        def dwin(h, r):
            return dp.at[dhalf(core), dcols(r, h)]

        def finish(i):
            for h in range(2):
                ks[i][h].wait_recv()
                acc(dwin(h, order[i]), B["cr"].at[:, dcols(order[i], h)])

        rel, rl, rr, _ = bufs["c5"]
        g_own, z_own = lax.div(m, 2), lax.rem(m, 2) * 2
        for i, rb in enumerate(order):
            if on_z:

                @pl.loop(0, 2)
                def _(t):
                    part = dot(B["dk"][...], S["W"][:, pl.ds(pl.multiple_of(rb * 1024 + t * 512, 512), 512)])
                    for q in range(4):
                        w = pl.ds(pl.multiple_of(rb * 1024 + q % 2 * 512 + (t * 2 + q // 2) * 128, 128), 128)
                        dp[row0 : row0 + rows, w] = part[:, q * 128 : q * 128 + 128].astype(BF16)

            else:

                @pl.loop(0, 2)
                def _(t):
                    weights = [
                        S["W"][:, pl.ds(pl.multiple_of((t * 2 + j) * 1024 + rb * 256, 256), 256)] for j in range(2)
                    ]
                    part = dot(B["dk"][...], jnp.concatenate(weights, axis=1))
                    for q in range(4):
                        w = pl.ds(pl.multiple_of((q % 2 * 4 + rb) * 512 + (t * 2 + q // 2) * 128, 128), 128)
                        dp[row0 : row0 + rows, w] = part[:, q * 128 : q * 128 + 128].astype(BF16)

            for t in range(2):
                mine = z_own + t == rb if on_z else lax.rem(g_own, 4) == rb

                @pl.when(mine)
                def _():
                    w = cols((z_own + t) * 8 + g_own if on_z else g_own * 4 + z_own + t, 128)
                    dp[row0 : row0 + rows, w] = (
                        f32(dp[row0 : row0 + rows, w]) + f32(S["hg"][row0 : row0 + rows, t * 128 : t * 128 + 128])
                    ).astype(BF16)

            ks.append(
                [send(dp.at[dhalf(1 - core), dcols(rb, h)], B["cr"].at[:, dcols(rb, h)], cp) for h in range(2)]
            )
            yield "back"
            if i == 1:
                finish(0)
                a = send(dwin(0, order[0]), rel.at[0], big_dev[0])
                b = send(dwin(1, order[0]), rel.at[1], big_dev[1])
            if i == 2:
                finish(1)
                c1 = send(dwin(1, order[1]), rl.at[1], big_dev[0])
            if i == 3:
                finish(2)
                d0 = send(dwin(0, order[2]), rr.at[0], big_dev[1])
        total = yield from rs_tail(dwin, bufs["c5"], big, big_dev, yl, lp, a, b, c1, d0, lambda: finish(3))
        B["E5"][...] = total.astype(BF16)
        total = yield from rs_far(
            lambda h, r: B["E5"].at[pl.ds(pl.multiple_of(h * r4, r4), r4), cols(r, 128)], B["e5"], yh, small, far_small
        )
        dt = B["dt"]
        dt[quarter(core, yh), cols(z, 128)] = total.astype(BF16)
        yield from ag_far(lambda h, r: dt.at[quarter(core, h), cols(r, 128)], yh, z, far_z)
        k = send(dt.at[half(core)], dt.at[half(core)], cp)
        yield
        k.wait_recv()
        keep = net.copy(dt.at[pl.ds(m * r16, r16)], B["own"])
        for n, w in TILES:
            part = dot_t(dt[...], S["td"][n : n + w, :])
            for j in range(8):
                B["G7"][j, :, n : n + w] = part[j * r8 : (j + 1) * r8].astype(BF16)
        more = rs_far(lambda h, r: B["G7"].at[h * 4 + r], B["c7"], yl, x, far_g)
        next(more)

        def gather_rows(out, left, right):
            first = once(out)
            for n, w in TILES:
                part = contract_first(left[:, n : n + w], right)
                if first:
                    outs[out][n : n + w, :] = part
                else:
                    outs[out][n : n + w, :] += part

        gather_rows(3, hid[...].reshape(rows, FL), dt[...])
        yield
        total = yield from more
        gh, dgu = B["gh"], B["dgu"]
        gh[g] = total.astype(BF16)
        yield from ag_far(lambda h, r: gh.at[h * 4 + r], yl, x, far_g)
        for i in range(2):
            dgu[i] = (f32(gh[...]) * f32(ab[i])).astype(BF16).reshape(rows, FL)
        part = dot(dgu[0], S["tg"][...]) + dot(dgu[1], S["tu"][...])
        X9 = B["X9"]
        for i in range(16):
            X9[i % 2, i // 8, i // 2 % 4] = part[i * r16 : (i + 1) * r16].astype(BF16)
        k = send(X9.at[1 - core], B["X9r"], cp)
        gather_rows(1, dgu[0], B["tok"][...])
        yield
        k.wait_recv()
        acc(X9.at[core], B["X9r"])
        more = rs_far(lambda h, r: X9.at[core, h, r], B["c9"], yh, z, far_z)
        next(more)
        gather_rows(2, dgu[1], B["tok"][...])
        yield
        total = yield from more
        keep.wait()
        outs[0][sum(FINAL[:c]) : sum(FINAL[: c + 1]), :] = (f32(B["own"][...]) + total).astype(BF16)

    gens = {"c": gather_cot(), "h": head_hidden()} | {str(c): chunk(c) for c in range(len(ROWS))}

    def step(gen):
        return next(gen, "end")

    for c in range(len(ROWS)):
        step(gens[str(c)])
    pl.semaphore_wait(barrier, len(near))
    for name in "".join(ORDER):
        step(gens[name])
    for gen in gens.values():
        while step(gen) != "end":
            pass
    for copy in net.sent:
        copy.wait_send()


def body(tokens, trunk_gate, trunk_up, trunk_down, head_gate, head_up, head_down, head_grads):
    names, shapes = layout()
    grad_x, grad_gate, grad_up, grad_down = pl.pallas_call(
        functools.partial(kernel, names),
        out_shape=[
            pltpu.VMEM((sum(FINAL), CW), BF16),
            pltpu.VMEM((FL, CW), F32),
            pltpu.VMEM((FL, CW), F32),
            pltpu.VMEM((FL, CW), F32),
        ],
        in_specs=[pl.BlockSpec(memory_space=pl.ANY)] * 8,
        out_specs=[pl.BlockSpec(memory_space=pltpu.VMEM)] * 4,
        scratch_shapes=[
            *shapes,
            pltpu.SemaphoreType.DMA((N_SEM,)),
            pltpu.SemaphoreType.DMA((N_SEM,)),
            pltpu.SemaphoreType.DMA((220,)),
        ],
        compiler_params=pltpu.CompilerParams(
            collective_id=0, has_side_effects=True, vmem_limit_bytes=62500000
        ),
    )(
        tokens,
        trunk_gate.T,
        trunk_up.T,
        trunk_down,
        head_gate[0].T,
        head_up[0].T,
        head_down[0],
        head_grads[0],
    )
    return grad_x, grad_gate.T, grad_up.T, grad_down


def solution(mesh):
    return jax.shard_map(
        body,
        mesh=mesh,
        in_specs=(
            P(None, "group"),
            P("group", "mp"),
            P("group", "mp"),
            P("mp", "group"),
            P("group", None, "mp"),
            P("group", None, "mp"),
            P("group", "mp", None),
            P("group", None, "mp"),
        ),
        out_specs=(P("mp", "group"), P("group", "mp"), P("group", "mp"), P("mp", "group")),
        check_vma=False,
    )
```

profile of v0, /device:TPU:0, one launch (start us, length us, event | category | flops | bytes accessed | tf_op | source)
XLA Modules:
  0.0 162.3 jit_solution(14542745162411754844)
XLA Ops:
  0.6 157.7 %shard_map.111 = (bf16[40,512]{1,0:T(8,128)(2,1)S(1)}, f32[688,512]{1,0:T(8,128)S(1)}, f32[688,512]{1,0:T(8,128)S(1)}, f32[688,512]{1,0:T(8,128)S(1)}) custom-call(bf16[640,512]{1,0:T(8,128)(2,1)} %refs_0_.1, bf16[688,512]{1,0:T(8,128)(2,1)} %bitcast.17, bf16[688,512]{1,0:T(8,128)(2,1)} %bitcast.18, bf16[688,512]{1,0:T(8,128)(2,1)} %refs_3_.1, ...), custom_call_target="tpu_custom_call" | custom-call | tf_op jit(solution)/shard_map/pallas_call | solution.py:584
  158.4 0.6 copy.16
  159.0 1.1 copy.17
  160.1 1.1 copy.18
  161.2 1.1 copy.19
where the time goes:
time: 163 us; the launch traced here: 162 us
  Pallas kernels  158 us (97%)
  local copies, waits for them, and re-layouts  3.88 us (2%)
    pallas_call x1, Pallas kernels, body(): pl.pallas_call(functools.partial(kernel, names), out_shape=[pltpu.VMEM((s...  158 us
    unnamed x4, local copies, waits for them, and re-layouts  3.88 us

commit v1 on v0

--- a/solution.py
+++ b/solution.py
@@ -80,8 +80,8 @@
 )
 N_SEM = 420
 ORDER = (
-    "0c10102c10210120c1200211c2022102c10hh2021hh0hh10001001210110",
-    "12010212012212012202122012120012102210210212102",
+    "0c10102c10210120c1200211c2022102c10h2021h0h10001001210110120",
+    "10212012212012202122012120012102210210212102",
 )
 
 
@@ -333,12 +333,10 @@
 
     def head_hidden():
         w_hd.wait()
-        row = 0
-        for rows in ROWS:
-            for n, w in ((0, 512), (512, 176)):
-                S["ghid"][row : row + rows, n : n + w] = dot_t(S["cot"][row : row + rows, :], S["Wd"][n : n + w, :])
-                yield
-            row += rows
+        for n, w in TILES:
+            for row in (0, 320):
+                S["ghid"][row : row + 320, n : n + w] = dot_t(S["cot"][row : row + 320, :], S["Wd"][n : n + w, :])
+            yield
 
     reached = set()
 

time: 163 us -> 162 us (level)
  no operation moved by 1% of the time
where the time goes in v1:
time: 162 us; the launch traced here: 161 us
  Pallas kernels  157 us (97%)
  local copies, waits for them, and re-layouts  3.88 us (2%)
    pallas_call x1, Pallas kernels, body(): pl.pallas_call(functools.partial(kernel, names), out_shape=[pltpu.VMEM((s...  157 us
    unnamed x4, local copies, waits for them, and re-layouts  3.88 us

profile of v1, /device:TPU:0, one launch (start us, length us, event | category | flops | bytes accessed | tf_op | source)
XLA Modules:
  0.0 161.1 jit_solution(1187422637810611707)
XLA Ops:
  0.6 156.6 %shard_map.111 = (bf16[40,512]{1,0:T(8,128)(2,1)S(1)}, f32[688,512]{1,0:T(8,128)S(1)}, f32[688,512]{1,0:T(8,128)S(1)}, f32[688,512]{1,0:T(8,128)S(1)}) custom-call(bf16[640,512]{1,0:T(8,128)(2,1)} %refs_0_.1, bf16[688,512]{1,0:T(8,128)(2,1)} %bitcast.17, bf16[688,512]{1,0:T(8,128)(2,1)} %bitcast.18, bf16[688,512]{1,0:T(8,128)(2,1)} %refs_3_.1, ...), custom_call_target="tpu_custom_call" | custom-call | tf_op jit(solution)/shard_map/pallas_call | solution.py:582
  157.2 0.6 copy.16
  157.8 1.1 copy.17
  158.9 1.1 copy.18
  160.0 1.1 copy.19
